TPU v7x, 256 devices: a whole 4x4x8 slice. The times are simulated.
256 devices in a mesh: seq: 32 (over x, z), tp: 4 (over y), lat: 2 (over core).
Axes of the slice: x: 4, y: 4, z: 8, core: 2. Of those that a mesh axis runs over, the one named last changes fastest.
Arguments:
- tokens: bfloat16 [24576, 8192], P(('seq', 'lat'), 'tp'), may hold values from -6 to 6
- active: int32 [24576, 4], P(('seq', 'lat')), may hold values from 0 to 255, all different within a row; in each aligned block of 384 rows (0 to 383, 384 to 767, ...) at most 9 rows name the same one
- placement_map: int32 [256], replicated, may hold values from 0 to 255, each once
- enc_weight: bfloat16 [8192, 32768], P('tp', ('seq', 'lat')), may hold values from -0.0625 to 0.0625
- enc_bias: float32 [32768], P(('seq', 'lat')), may hold values from -3 to 3
- dec_weight: bfloat16 [32768, 8192], P(('seq', 'lat'), 'tp'), may hold values from -0.375 to 0.375
- dec_bias: float32 [8192], P('tp'), may hold values from -3 to 3
Outputs:
- recon: bfloat16 [24576, 8192], P(('seq', 'lat'), 'tp')
Inputs may be any that keep to these rules, and one draw needn't show every extreme that they name: `active`: the 4 blocks of one token are different. Among the rows of one device (aligned blocks of 384 rows) no block is named more than 9 times, and some block is named exactly 9 times. `placement_map`: each column block appears once.
All inputs are finite; a program needn't handle non-finite values.
Results may differ from a plain program's by a relative error of at most 0.0061.
Values may be sent and summed in bfloat16 or wider, within the bound.
A program may use at most 128 MiB of HBM per device.

v0:
```python
import jax
import jax.numpy as jnp
from jax import lax
from jax.sharding import PartitionSpec as P


def local(tokens, active, placement_map, enc_weight, enc_bias, dec_weight, dec_bias):
    rows, width = tokens.shape
    top = active.shape[1]
    nblocks = placement_map.shape[0]
    seq_count = lax.axis_size("seq")
    lat_count = lax.axis_size("lat")
    owners = seq_count * lat_count
    local_blocks = nblocks // owners
    block_width = enc_bias.shape[0] // local_blocks
    capacity = 3 * rows * top // (2 * nblocks)
    centered = (tokens.astype(jnp.float32) - dec_bias[None, :]).astype(jnp.bfloat16)
    block_ids = jnp.arange(nblocks, dtype=jnp.int32)
    matches = (active[:, :, None] == block_ids[None, None, :]).astype(jnp.int32)
    position = jnp.sum(matches * placement_map[None, None, :], axis=2).reshape(-1)
    pos_hot = (position[:, None] == block_ids[None, :]).astype(jnp.int32)
    rank = jnp.sum((jnp.cumsum(pos_hot, axis=0) - 1) * pos_hot, axis=1)
    target = position * capacity + rank
    pair_row = jnp.arange(rows * top, dtype=jnp.int32) // top
    slot_row = jnp.zeros((nblocks * capacity,), jnp.int32).at[target].set(pair_row)
    filled = jnp.zeros((nblocks * capacity,), jnp.bool_).at[target].set(True)
    outgoing = jnp.where(filled[:, None], centered[slot_row], jnp.zeros((), jnp.bfloat16))
    outgoing = outgoing.reshape(owners, local_blocks, capacity, width)
    enc_blocks = enc_weight.reshape(width, local_blocks, block_width)
    bias_blocks = enc_bias.reshape(local_blocks, block_width)
    dec_blocks = dec_weight.reshape(local_blocks, block_width, width)
    preact = jnp.einsum(
        "sbcd,dbh->sbch",
        lax.all_to_all(outgoing, ("seq", "lat"), split_axis=0, concat_axis=0, tiled=True),
        enc_blocks,
        preferred_element_type=jnp.float32,
    )
    summed = lax.psum(preact, "tp")
    codes = jnp.maximum(summed + bias_blocks[None, :, None, :], 0.0).astype(jnp.bfloat16)
    returned = lax.all_to_all(
        jnp.einsum("sbch,bhd->sbcd", codes, dec_blocks, preferred_element_type=jnp.float32).astype(
            jnp.bfloat16
        ),
        ("seq", "lat"),
        split_axis=0,
        concat_axis=0,
        tiled=True,
    )
    returned = returned.reshape(nblocks * capacity, width)
    contrib = returned[target].reshape(rows, top, width).astype(jnp.float32)
    return (jnp.sum(contrib, axis=1) + dec_bias[None, :]).astype(jnp.bfloat16)


def solution(mesh):
    return jax.shard_map(
        local,
        mesh=mesh,
        in_specs=(
            P(("seq", "lat"), "tp"),
            P(("seq", "lat"), None),
            P(),
            P("tp", ("seq", "lat")),
            P(("seq", "lat")),
            P(("seq", "lat"), "tp"),
            P("tp"),
        ),
        out_specs=P(("seq", "lat"), "tp"),
        check_vma=False,
    )
```

profile of v0, /device:TPU:1, one launch (start us, length us, event | category | flops | bytes accessed | tf_op | source)
XLA Modules:
  0.0 689.2 jit_solution(1939051492768150350)
XLA Ops:
  6.5 0.0 copy-start
  6.5 1.4 select_reduce_fusion
  7.9 0.1 copy.29
  8.0 0.1 eq.45
  8.2 0.1 eq.41
  8.4 0.1 copy.31
  8.5 0.3 fusion.3
  8.8 0.0 copy-start.2
  8.8 1.3 copy-done.2
  10.2 1.8 add_add_fusion
  12.0 0.0 copy-start.3
  12.1 2.1 copy.32
  14.1 0.1 copy.28
  14.3 0.2 mul.31
  14.4 1.9 fusion.5
  16.4 6.4 scatter_custom_fusion.1
  22.8 0.0 copy-done.3
  22.8 2.9 subtract_convert_fusion
  25.7 20.0 %gather_fusion = bf16[2304,2048]{1,0:T(8,128)(2,1)} fusion(bf16[384,2048]{1,0:T(8,128)(2,1)} %subtract_convert_fusion, s32[3072]{0:T(1024)S(1)} %pad_clamp_fusion), kind=kCustom, calls=%fused_computation | custom fusion | bytes 18883584 | tf_op jit(solution)/shard_map/gather | solution.py:27
  45.7 15.1 %gather.9 = bf16[64,4,9,2048]{3,2,1,0:T(8,128)(2,1)} reshape(bf16[2304,2048]{1,0:T(8,128)(2,1)} %gather_fusion) | data formatting | bytes 18874368 | tf_op jit(solution)/shard_map/gather | solution.py:27
  60.8 11.2 %scatter_custom_fusion = pred[2304]{0:T(1024)(128)(4,1)S(1)} fusion(s32[1536]{0:T(1024)S(1)} %fusion.17, pred[1536]{0:T(1024)(128)(4,1)S(1)} %broadcast.82, pred[]{:T(512)} %constant.16.clone.1), kind=kCustom, calls=%fused_computation.40 | custom fusion | bytes 2305 | tf_op jit(solution)/shard_map/scatter | solution.py:26
  72.0 0.2 broadcast_in_dim.35
  72.2 8.3 %broadcast_select_fusion = bf16[64,4,9,2048]{3,2,1,0:T(8,128)(2,1)S(1)} fusion(bf16[64,4,9,2048]{3,2,1,0:T(8,128)(2,1)} %gather.9, pred[64,4,9]{2,1,0:T(4,128)(4,1)S(1)} %broadcast_in_dim.35), kind=kLoop, calls=%fused_computation.4 | loop fusion | flops 4718592 | bytes 18876672 | tf_op jit(solution)/shard_map/jit(_where)/select_n | solution.py:27
  80.5 19.6 %copy.33 = bf16[64,4,9,2048]{3,1,2,0:T(4,128)(2,1)} copy(bf16[64,4,9,2048]{3,2,1,0:T(8,128)(2,1)S(1)} %broadcast_select_fusion) | data formatting | bytes 18874368 | tf_op jit(solution)/shard_map/jit(_where)/select_n | solution.py:27
  100.1 13.2 %all-to-all-start = ((bf16[64,4,9,2048]{3,1,2,0:T(4,128)(2,1)}), bf16[64,4,9,2048]{3,1,2,0:T(4,128)(2,1)}, u32[]{:S(2)}, u32[]{:S(2)}) async-start(bf16[64,4,9,2048]{3,1,2,0:T(4,128)(2,1)} %copy.33), calls=%async_computation | async-start | bytes 18874368 | tf_op jit(solution)/shard_map/all_to_all | solution.py:34
  113.2 0.3 all-reduce.2.cloned.1.call-start
  113.5 4.0 reshape.73
  117.5 204.0 %all-to-all-done = bf16[64,4,9,2048]{3,1,2,0:T(4,128)(2,1)} async-done(((bf16[64,4,9,2048]{3,1,2,0:T(4,128)(2,1)}), bf16[64,4,9,2048]{3,1,2,0:T(4,128)(2,1)}, u32[]{:S(2)}, u32[]{:S(2)}) %all-to-all-start) | async-done | bytes 9437216 | tf_op jit(solution)/shard_map/all_to_all | solution.py:34
  321.5 0.0 copy-start.4
  321.5 10.5 %fusion.6 = f32[64,4,9,128]{3,0,2,1:T(8,128)} fusion(bf16[2048,4,128,1]{2,1,0,3:T(4,128)(2,1)} %bitcast.22, bf16[64,4,9,2048]{3,1,2,0:T(4,128)(2,1)} %all-to-all-done), kind=kOutput, calls=%fused_computation.20 | convolution fusion | flops 1207959552 | bytes 12713984 | tf_op jit(solution)/shard_map/sbcd,dbh->sbch/dot_general | solution.py:32
  332.0 0.0 all-reduce.2.cloned.1.call-update
  332.0 47.5 %all-reduce.2.cloned.1.call-done = f32[64,4,9,128]{3,0,2,1:T(8,128)} async-done(((f32[64,4,9,128]{3,0,2,1:T(8,128)}), f32[64,4,9,128]{3,0,2,1:T(8,128)}) %all-reduce.2.cloned.1.call-update) | async-done | bytes 1179664 | tf_op jit(solution)/shard_map/psum | solution.py:38
  379.5 0.0 copy-done
  379.5 0.0 copy-done.4
  379.5 4.1 convert_bitcast_fusion
  383.6 7.3 %copy.36 = bf16[64,4,9,2048]{3,1,2,0:T(4,128)(2,1)} copy(bf16[64,4,9,2048]{3,0,2,1:T(8,128)(2,1)S(1)} %convert_bitcast_fusion) | data formatting | bytes 18874368 | tf_op jit(solution)/shard_map/convert_element_type | solution.py:41
  390.9 11.9 %all-to-all-start.1 = ((bf16[64,4,9,2048]{3,1,2,0:T(4,128)(2,1)}), bf16[64,4,9,2048]{3,1,2,0:T(4,128)(2,1)}, u32[]{:S(2)}, u32[]{:S(2)}) async-start(bf16[64,4,9,2048]{3,1,2,0:T(4,128)(2,1)} %copy.36), calls=%async_computation.1 | async-start | bytes 18874368 | tf_op jit(solution)/shard_map/all_to_all | solution.py:40
  402.9 208.2 %all-to-all-done.1 = bf16[64,4,9,2048]{3,1,2,0:T(4,128)(2,1)} async-done(((bf16[64,4,9,2048]{3,1,2,0:T(4,128)(2,1)}), bf16[64,4,9,2048]{3,1,2,0:T(4,128)(2,1)}, u32[]{:S(2)}, u32[]{:S(2)}) %all-to-all-start.1) | async-done | bytes 9437216 | tf_op jit(solution)/shard_map/all_to_all | solution.py:40
  611.1 10.7 %copy.37 = bf16[64,4,9,2048]{3,2,1,0:T(8,128)(2,1)} copy(bf16[64,4,9,2048]{3,1,2,0:T(4,128)(2,1)} %all-to-all-done.1) | data formatting | bytes 18874368 | tf_op jit(solution)/shard_map/all_to_all | solution.py:40
  621.8 15.8 %reshape.75 = bf16[2304,2048]{1,0:T(8,128)(2,1)} reshape(bf16[64,4,9,2048]{3,2,1,0:T(8,128)(2,1)} %copy.37) | data formatting | bytes 18874368 | tf_op jit(solution)/shard_map/reshape | solution.py:49
  637.6 17.6 %gather_fusion.1 = bf16[1536,2048]{1,0:T(8,128)(2,1)} fusion(bf16[2304,2048]{1,0:T(8,128)(2,1)} %reshape.75, s32[2048]{0:T(1024)S(1)} %pad_clamp_fusion.1), kind=kCustom, calls=%fused_computation.1 | custom fusion | bytes 12589056 | tf_op jit(solution)/shard_map/gather | solution.py:50
  655.2 11.9 %reshape.76 = f32[384,4,2048]{2,1,0:T(4,128)} reshape(bf16[1536,2048]{1,0:T(8,128)(2,1)} %gather_fusion.1) | data formatting | bytes 18874368 | tf_op jit(solution)/shard_map/convert_element_type | solution.py:50
  667.1 0.0 copy-start.1
  667.1 11.9 %reduce_sum.32 = f32[384,2048]{1,0:T(8,128)} reduce(f32[384,4,2048]{2,1,0:T(4,128)} %reshape.76, f32[]{:T(128)} %constant.42.clone.1), dimensions={1}, to_apply=%region_7.8 | reduce | flops 2359296 | bytes 15728644 | tf_op jit(solution)/shard_map/reduce_sum | solution.py:51
  679.0 3.4 add_convert_fusion
  682.4 0.0 copy-done.1
  (9 shorter events, 0.1 us)
Async XLA Ops:
  6.5 373.0 %copy-start = (bf16[512,2048]{1,0:T(8,128)(2,1)S(1)}, bf16[512,2048]{1,0:T(8,128)(2,1)}, u32[]{:S(2)}) copy-start(bf16[512,2048]{1,0:T(8,128)(2,1)} %param.12) | copy-start | bytes 6291460
  8.8 1.4 copy-start.2
  12.0 10.7 %copy-start.3 = (f32[2048]{0:T(1024)S(1)}, f32[2048]{0:T(1024)}, u32[]{:S(2)}) copy-start(f32[2048]{0:T(1024)} %param.13) | copy-start | bytes 24580
  100.1 221.4 %all-to-all-start = ((bf16[64,4,9,2048]{3,1,2,0:T(4,128)(2,1)}), bf16[64,4,9,2048]{3,1,2,0:T(4,128)(2,1)}, u32[]{:S(2)}, u32[]{:S(2)}) async-start(bf16[64,4,9,2048]{3,1,2,0:T(4,128)(2,1)} %copy.33), calls=%async_computation | async-start | bytes 18874368 | tf_op jit(solution)/shard_map/all_to_all | solution.py:34
  113.2 266.3 %all-reduce.2.cloned.1.call-start = ((), (), s32[]{:S(2)}) async-start(), calls=%async_computation.2 | async-start | bytes 2359296 | tf_op jit(solution)/shard_map/psum | solution.py:38
  321.5 58.0 %copy-start.4 = (f32[512]{0:T(512)S(1)}, f32[512]{0:T(512)}, u32[]{:S(2)}) copy-start(f32[512]{0:T(512)} %param.11) | copy-start | bytes 6148
  390.9 220.2 %all-to-all-start.1 = ((bf16[64,4,9,2048]{3,1,2,0:T(4,128)(2,1)}), bf16[64,4,9,2048]{3,1,2,0:T(4,128)(2,1)}, u32[]{:S(2)}, u32[]{:S(2)}) async-start(bf16[64,4,9,2048]{3,1,2,0:T(4,128)(2,1)} %copy.36), calls=%async_computation.1 | async-start | bytes 18874368 | tf_op jit(solution)/shard_map/all_to_all | solution.py:40
  667.1 15.3 %copy-start.1 = (bf16[512,2048]{1,0:T(8,128)(2,1)S(1)}, bf16[512,2048]{1,0:T(8,128)(2,1)}, u32[]{:S(2)}) copy-start(bf16[512,2048]{1,0:T(8,128)(2,1)} %param.12) | copy-start | bytes 6291460
Sparse Core Ops, SparseCore 0:
  332.1 47.3 all-reduce.1
where the time goes:
time: 691 us; the launch traced here: 689 us
  waiting for transfers between devices  460 us (67%)
  local copies, waits for them, and re-layouts  144 us (21%)
  other arithmetic  32 us (5%)
  starting transfers between devices  25.3 us (4%)
  matrix products  14.6 us (2%)
  between operations  13.6 us (2%)
    all_to_all x1, waiting for transfers between devices, local(): lax.all_to_all(jnp.einsum('sbch,bhd->sbcd', codes, dec_blocks, preferred_...  208 us
    all_to_all x1, waiting for transfers between devices, local(): lax.all_to_all(outgoing, ('seq', 'lat'), split_axis=0, concat_axis=0, til...  204 us
    psum x1, waiting for transfers between devices, local(): summed = lax.psum(preact, 'tp')  47.5 us
    gather x2, local copies, waits for them, and re-layouts, local(): centered[slot_row]  35 us
    select_n x1, local copies, waits for them, and re-layouts, local(): jnp.where(filled[:, None], centered[slot_row], jnp.zeros((), jnp.bfloat16))  19.6 us
    gather x1, local copies, waits for them, and re-layouts, local(): contrib = returned[target].reshape(rows, top, width).astype(jnp.float32)  17.6 us
    reshape x1, local copies, waits for them, and re-layouts, local(): returned = returned.reshape(nblocks * capacity, width)  15.8 us
  transfers between devices with their start and end apart: 3, of which 3 were waited for; matrix products, arithmetic and copies ran while one was open for 1% of the time, Pallas kernels for 0%

commit v1 on v0

--- a/solution.py
+++ b/solution.py
@@ -35,7 +35,9 @@
         enc_blocks,
         preferred_element_type=jnp.float32,
     )
-    summed = lax.psum(preact, "tp")
+    summed = preact
+    for hop in (1, 2):
+        summed = summed + lax.ppermute(summed, "tp", [(dev, dev ^ hop) for dev in range(4)])
     codes = jnp.maximum(summed + bias_blocks[None, :, None, :], 0.0).astype(jnp.bfloat16)
     returned = lax.all_to_all(
         jnp.einsum("sbch,bhd->sbcd", codes, dec_blocks, preferred_element_type=jnp.float32).astype(

time: 691 us -> 680 us (0.984)
  between operations: 13.6 us -> 0.19 us
    ppermute x0 -> x2, waiting for transfers between devices: none -> 52.3 us  [local(): lax.ppermute(summed, 'tp', [(dev, dev ^ hop) for dev in range(4)])]
    psum x1 -> x0, waiting for transfers between devices: 47.5 us -> none  [local(): summed = lax.psum(preact, 'tp')]
  transfers between devices with their start and end apart: 3 -> 4, of which waited for: 3 -> 4; matrix products, arithmetic and copies ran while one was open for 1% -> 1% of each run, Pallas kernels for 0% -> 0%
where the time goes in v1:
time: 680 us; the launch traced here: 679 us
  waiting for transfers between devices  465 us (68%)
  local copies, waits for them, and re-layouts  144 us (21%)
  other arithmetic  32.2 us (5%)
  starting transfers between devices  24.1 us (4%)
  matrix products  13.4 us (2%)
    all_to_all x1, waiting for transfers between devices, local(): lax.all_to_all(jnp.einsum('sbch,bhd->sbcd', codes, dec_blocks, preferred_...  208 us
    all_to_all x1, waiting for transfers between devices, local(): lax.all_to_all(outgoing, ('seq', 'lat'), split_axis=0, concat_axis=0, til...  204 us
    ppermute x2, waiting for transfers between devices, local(): lax.ppermute(summed, 'tp', [(dev, dev ^ hop) for dev in range(4)])  52.3 us
    gather x2, local copies, waits for them, and re-layouts, local(): centered[slot_row]  35 us
    select_n x1, local copies, waits for them, and re-layouts, local(): jnp.where(filled[:, None], centered[slot_row], jnp.zeros((), jnp.bfloat16))  19.6 us
    gather x1, local copies, waits for them, and re-layouts, local(): contrib = returned[target].reshape(rows, top, width).astype(jnp.float32)  17.6 us
    reshape x1, local copies, waits for them, and re-layouts, local(): returned = returned.reshape(nblocks * capacity, width)  15.8 us
  transfers between devices with their start and end apart: 4, of which 4 were waited for; matrix products, arithmetic and copies ran while one was open for 1% of the time, Pallas kernels for 0%

profile of v1, /device:TPU:1, one launch (start us, length us, event | category | flops | bytes accessed | tf_op | source)
XLA Modules:
  0.0 678.6 jit_solution(11748574870754439867)
XLA Ops:
  0.0 0.0 copy-start
  0.0 1.4 select_reduce_fusion
  1.4 0.1 copy.32
  1.5 0.1 eq.45
  1.7 0.1 eq.41
  1.8 0.1 copy.34
  1.9 0.3 fusion.3
  2.3 0.0 copy-start.2
  2.3 1.3 copy-done.2
  3.7 1.8 add_add_fusion
  5.5 0.0 copy-start.3
  5.5 2.1 copy.35
  7.6 0.1 copy.31
  7.7 0.2 mul.31
  7.9 1.9 fusion.5
  9.8 6.4 scatter_custom_fusion.1
  16.2 0.0 copy-done.3
  16.2 2.9 subtract_convert_fusion
  19.2 20.0 %gather_fusion = bf16[2304,2048]{1,0:T(8,128)(2,1)} fusion(bf16[384,2048]{1,0:T(8,128)(2,1)} %subtract_convert_fusion, s32[3072]{0:T(1024)S(1)} %pad_clamp_fusion), kind=kCustom, calls=%fused_computation | custom fusion | bytes 18883584 | tf_op jit(solution)/shard_map/gather | solution.py:27
  39.2 15.1 %gather.9 = bf16[64,4,9,2048]{3,2,1,0:T(8,128)(2,1)} reshape(bf16[2304,2048]{1,0:T(8,128)(2,1)} %gather_fusion) | data formatting | bytes 18874368 | tf_op jit(solution)/shard_map/gather | solution.py:27
  54.2 11.2 %scatter_custom_fusion = pred[2304]{0:T(1024)(128)(4,1)S(1)} fusion(s32[1536]{0:T(1024)S(1)} %fusion.17, pred[1536]{0:T(1024)(128)(4,1)S(1)} %broadcast.82, pred[]{:T(512)} %constant.16.clone.1), kind=kCustom, calls=%fused_computation.40 | custom fusion | bytes 2305 | tf_op jit(solution)/shard_map/scatter | solution.py:26
  65.4 0.2 broadcast_in_dim.35
  65.7 8.3 %broadcast_select_fusion = bf16[64,4,9,2048]{3,2,1,0:T(8,128)(2,1)S(1)} fusion(bf16[64,4,9,2048]{3,2,1,0:T(8,128)(2,1)} %gather.9, pred[64,4,9]{2,1,0:T(4,128)(4,1)S(1)} %broadcast_in_dim.35), kind=kLoop, calls=%fused_computation.4 | loop fusion | flops 4718592 | bytes 18876672 | tf_op jit(solution)/shard_map/jit(_where)/select_n | solution.py:27
  74.0 19.6 %copy.36 = bf16[64,4,9,2048]{3,1,2,0:T(4,128)(2,1)} copy(bf16[64,4,9,2048]{3,2,1,0:T(8,128)(2,1)S(1)} %broadcast_select_fusion) | data formatting | bytes 18874368 | tf_op jit(solution)/shard_map/jit(_where)/select_n | solution.py:27
  93.5 13.2 %all-to-all-start = ((bf16[64,4,9,2048]{3,1,2,0:T(4,128)(2,1)}), bf16[64,4,9,2048]{3,1,2,0:T(4,128)(2,1)}, u32[]{:S(2)}, u32[]{:S(2)}) async-start(bf16[64,4,9,2048]{3,1,2,0:T(4,128)(2,1)} %copy.36), calls=%async_computation | async-start | bytes 18874368 | tf_op jit(solution)/shard_map/all_to_all | solution.py:34
  106.7 4.0 reshape.73
  110.7 204.3 %all-to-all-done = bf16[64,4,9,2048]{3,1,2,0:T(4,128)(2,1)} async-done(((bf16[64,4,9,2048]{3,1,2,0:T(4,128)(2,1)}), bf16[64,4,9,2048]{3,1,2,0:T(4,128)(2,1)}, u32[]{:S(2)}, u32[]{:S(2)}) %all-to-all-start) | async-done | bytes 9437216 | tf_op jit(solution)/shard_map/all_to_all | solution.py:34
  315.0 10.6 %fusion.6 = f32[64,4,9,128]{3,0,2,1:T(8,128)S(1)} fusion(bf16[2048,4,128,1]{2,1,0,3:T(4,128)(2,1)} %bitcast.22, bf16[64,4,9,2048]{3,1,2,0:T(4,128)(2,1)} %all-to-all-done), kind=kOutput, calls=%fused_computation.20 | convolution fusion | flops 1207959552 | bytes 12713984 | tf_op jit(solution)/shard_map/sbcd,dbh->sbch/dot_general | solution.py:32
  325.5 0.0 copy-start.4
  325.5 1.4 collective-permute-start
  326.9 26.6 %collective-permute-done = f32[64,4,9,128]{3,0,2,1:T(8,128)S(1)} collective-permute-done((f32[64,4,9,128]{3,0,2,1:T(8,128)S(1)}, f32[64,4,9,128]{3,0,2,1:T(8,128)S(1)}, u32[]{:S(2)}, u32[]{:S(2)}) %collective-permute-start) | collective-permute-done | bytes 1179680 | tf_op jit(solution)/shard_map/ppermute | solution.py:40
  353.6 0.2 add.58
  353.7 3.0 collective-permute-start.1
  356.7 25.7 %collective-permute-done.1 = f32[64,4,9,128]{3,0,2,1:T(8,128)S(1)} collective-permute-done((f32[64,4,9,128]{3,0,2,1:T(8,128)S(1)}, f32[64,4,9,128]{3,0,2,1:T(8,128)S(1)}, u32[]{:S(2)}, u32[]{:S(2)}) %collective-permute-start.1) | collective-permute-done | bytes 1179680 | tf_op jit(solution)/shard_map/ppermute | solution.py:40
  382.4 0.0 copy-done
  382.4 0.0 copy-done.4
  382.4 2.8 convert_bitcast_fusion
  385.2 7.3 %copy.39 = bf16[64,4,9,2048]{3,1,2,0:T(4,128)(2,1)} copy(bf16[64,4,9,2048]{3,0,2,1:T(8,128)(2,1)S(1)} %convert_bitcast_fusion) | data formatting | bytes 18874368 | tf_op jit(solution)/shard_map/convert_element_type | solution.py:43
  392.5 6.5 all-to-all-start.1
  399.1 208.2 %all-to-all-done.1 = bf16[64,4,9,2048]{3,1,2,0:T(4,128)(2,1)} async-done(((bf16[64,4,9,2048]{3,1,2,0:T(4,128)(2,1)}), bf16[64,4,9,2048]{3,1,2,0:T(4,128)(2,1)}, u32[]{:S(2)}, u32[]{:S(2)}) %all-to-all-start.1) | async-done | bytes 9437216 | tf_op jit(solution)/shard_map/all_to_all | solution.py:42
  607.3 10.7 %copy.40 = bf16[64,4,9,2048]{3,2,1,0:T(8,128)(2,1)} copy(bf16[64,4,9,2048]{3,1,2,0:T(4,128)(2,1)} %all-to-all-done.1) | data formatting | bytes 18874368 | tf_op jit(solution)/shard_map/all_to_all | solution.py:42
  618.0 15.8 %reshape.75 = bf16[2304,2048]{1,0:T(8,128)(2,1)} reshape(bf16[64,4,9,2048]{3,2,1,0:T(8,128)(2,1)} %copy.40) | data formatting | bytes 18874368 | tf_op jit(solution)/shard_map/reshape | solution.py:51
  633.8 17.6 %gather_fusion.1 = bf16[1536,2048]{1,0:T(8,128)(2,1)} fusion(bf16[2304,2048]{1,0:T(8,128)(2,1)} %reshape.75, s32[2048]{0:T(1024)S(1)} %pad_clamp_fusion.1), kind=kCustom, calls=%fused_computation.1 | custom fusion | bytes 12589056 | tf_op jit(solution)/shard_map/gather | solution.py:52
  651.4 11.9 %reshape.76 = f32[384,4,2048]{2,1,0:T(4,128)} reshape(bf16[1536,2048]{1,0:T(8,128)(2,1)} %gather_fusion.1) | data formatting | bytes 18874368 | tf_op jit(solution)/shard_map/convert_element_type | solution.py:52
  663.3 0.0 copy-start.1
  663.3 11.9 %reduce_sum.32 = f32[384,2048]{1,0:T(8,128)} reduce(f32[384,4,2048]{2,1,0:T(4,128)} %reshape.76, f32[]{:T(128)} %constant.42.clone.1), dimensions={1}, to_apply=%region_6.7 | reduce | flops 2359296 | bytes 15728644 | tf_op jit(solution)/shard_map/reduce_sum | solution.py:53
  675.2 3.4 add_convert_fusion
  678.5 0.0 copy-done.1
  (9 shorter events, 0.1 us)
Async XLA Ops:
  0.0 382.4 %copy-start = (bf16[512,2048]{1,0:T(8,128)(2,1)S(1)}, bf16[512,2048]{1,0:T(8,128)(2,1)}, u32[]{:S(2)}) copy-start(bf16[512,2048]{1,0:T(8,128)(2,1)} %param.12) | copy-start | bytes 6291460
  2.3 1.4 copy-start.2
  5.5 10.7 %copy-start.3 = (f32[2048]{0:T(1024)S(1)}, f32[2048]{0:T(1024)}, u32[]{:S(2)}) copy-start(f32[2048]{0:T(1024)} %param.13) | copy-start | bytes 24580
  93.5 221.4 %all-to-all-start = ((bf16[64,4,9,2048]{3,1,2,0:T(4,128)(2,1)}), bf16[64,4,9,2048]{3,1,2,0:T(4,128)(2,1)}, u32[]{:S(2)}, u32[]{:S(2)}) async-start(bf16[64,4,9,2048]{3,1,2,0:T(4,128)(2,1)} %copy.36), calls=%async_computation | async-start | bytes 18874368 | tf_op jit(solution)/shard_map/all_to_all | solution.py:34
  325.5 56.8 %copy-start.4 = (f32[512]{0:T(512)S(1)}, f32[512]{0:T(512)}, u32[]{:S(2)}) copy-start(f32[512]{0:T(512)} %param.11) | copy-start | bytes 6148
  325.5 28.0 %collective-permute-start = (f32[64,4,9,128]{3,0,2,1:T(8,128)S(1)}, f32[64,4,9,128]{3,0,2,1:T(8,128)S(1)}, u32[]{:S(2)}, u32[]{:S(2)}) collective-permute-start(f32[64,4,9,128]{3,0,2,1:T(8,128)S(1)} %fusion.6), channel_id=1, source_target_pairs={{0,2},{2,0},{4,6},{6,4},{1,3},{3,1},{5,7},{7,5},{8,10},{10,8},{12,... | collective-permute-start | bytes 3538952 | tf_op jit(solution)/shard_map/ppermute | solution.py:40
  353.7 28.7 %collective-permute-start.1 = (f32[64,4,9,128]{3,0,2,1:T(8,128)S(1)}, f32[64,4,9,128]{3,0,2,1:T(8,128)S(1)}, u32[]{:S(2)}, u32[]{:S(2)}) collective-permute-start(f32[64,4,9,128]{3,0,2,1:T(8,128)S(1)} %add.58), channel_id=1, source_target_pairs={{0,4},{2,6},{4,0},{6,2},{1,5},{3,7},{5,1},{7,3},{8,12},{10,14},{12... | collective-permute-start | bytes 3538952 | tf_op jit(solution)/shard_map/ppermute | solution.py:40
  392.5 214.8 %all-to-all-start.1 = ((bf16[64,4,9,2048]{3,1,2,0:T(4,128)(2,1)}), bf16[64,4,9,2048]{3,1,2,0:T(4,128)(2,1)}, u32[]{:S(2)}, u32[]{:S(2)}) async-start(bf16[64,4,9,2048]{3,1,2,0:T(4,128)(2,1)} %copy.39), calls=%async_computation.1 | async-start | bytes 18874368 | tf_op jit(solution)/shard_map/all_to_all | solution.py:42
  663.3 15.3 %copy-start.1 = (bf16[512,2048]{1,0:T(8,128)(2,1)S(1)}, bf16[512,2048]{1,0:T(8,128)(2,1)}, u32[]{:S(2)}) copy-start(bf16[512,2048]{1,0:T(8,128)(2,1)} %param.12) | copy-start | bytes 6291460
